TPU v7x, 128 devices: a whole 4x4x4 slice. The times are simulated.
128 devices in a mesh: fsdp: 16 (over x_lo, y, core), tp: 8 (over x_hi, z).
Axes of the slice: x: 4 (x_hi: 2, x_lo: 2; x = x_hi * 2 + x_lo), y: 4, z: 4, core: 2. Of those that a mesh axis runs over, the one named last changes fastest.
Arguments:
- tokens: bfloat16 [16384, 2048], P(('fsdp', 'tp')), may hold values from -6 to 6
- grad_out: bfloat16 [16384, 2048], P(('fsdp', 'tp')), may hold values from -6 to 6
- adapter_ids: int32 [16], P('fsdp'), may hold values from 0 to 7
- first_gain: float32 [2048], replicated, may hold values from 0.1 to 1.9
- first_shift: float32 [2048], replicated, may hold values from -4 to 4
- joined_weight: bfloat16 [2048, 6144], P('fsdp', 'tp'), may hold values from -0.125 to 0.125
- joined_bias: float32 [6144], P('tp'), may hold values from -4 to 4
- dense_weight: bfloat16 [2048, 2048], P('tp', 'fsdp'), may hold values from -0.5 to 0.5
- dense_bias: float32 [2048], replicated, may hold values from -4 to 4
- second_gain: float32 [2048], replicated, may hold values from 0.1 to 1.9
- second_shift: float32 [2048], replicated, may hold values from -4 to 4
- up_weight: bfloat16 [2048, 8192], P('fsdp', 'tp'), may hold values from -0.125 to 0.125
- up_bias: float32 [8192], P('tp'), may hold values from -6 to 6
- down_weight: bfloat16 [8192, 2048], P('tp', 'fsdp'), may hold values from -0.125 to 0.125
- down_bias: float32 [2048], replicated, may hold values from -4 to 4
- joined_adapt_in: bfloat16 [8, 2048, 16], replicated, may hold values from -0.125 to 0.125
- joined_adapt_out: bfloat16 [8, 16, 6144], P(None, None, 'tp'), may hold values from -2 to 2
- dense_adapt_in: bfloat16 [8, 2048, 16], P(None, 'tp'), may hold values from -0.5 to 0.5
- dense_adapt_out: bfloat16 [8, 16, 2048], replicated, may hold values from -2 to 2
- up_adapt_in: bfloat16 [8, 2048, 16], replicated, may hold values from -0.125 to 0.125
- up_adapt_out: bfloat16 [8, 16, 8192], P(None, None, 'tp'), may hold values from -2 to 2
- down_adapt_in: bfloat16 [8, 8192, 16], P(None, 'tp'), may hold values from -0.125 to 0.125
- down_adapt_out: bfloat16 [8, 16, 2048], replicated, may hold values from -2 to 2
Outputs:
- layer_out: bfloat16 [16384, 2048], P(('fsdp', 'tp'))
- grad_tokens: float32 [16384, 2048], P(('fsdp', 'tp'))
- grad_joined_in: float32 [8, 2048, 16], replicated
- grad_joined_out: float32 [8, 16, 6144], P(None, None, 'tp')
- grad_dense_in: float32 [8, 2048, 16], P(None, 'tp')
- grad_dense_out: float32 [8, 16, 2048], replicated
- grad_up_in: float32 [8, 2048, 16], replicated
- grad_up_out: float32 [8, 16, 8192], P(None, None, 'tp')
- grad_down_in: float32 [8, 8192, 16], P(None, 'tp')
- grad_down_out: float32 [8, 16, 2048], replicated
All inputs are finite; a program needn't handle non-finite values.
Results may differ from a plain program's by a relative error of at most 0.02.
Values may be sent and summed in bfloat16 or wider, within the bound.
A program may use at most 128 MiB of HBM per device.

v0:
```python
import functools

import jax
import jax.numpy as jnp
from jax import lax
from jax.experimental import pallas as pl
from jax.experimental.pallas import tpu as pltpu
from jax.sharding import Mesh
from jax.sharding import PartitionSpec as P

HEADS = 32
EPSILON = 1e-05
MASKED = -1e30
AXES = ("xl", "y", "c", "xh", "z")
FSDP = ("xl", "y", "c")
TP = ("xh", "z")
PLANE = ("xl", "y", "xh")
MESH_ID = pl.DeviceIdType.MESH
ANY = pl.ANY
VMEM = pltpu.VMEM
DMA = pltpu.SemaphoreType.DMA
F32 = jnp.float32
BF16 = jnp.bfloat16
ORDER = (0, 3, 1, 2)
PICKS = dict(hot=(0, 128), joined_out=(128, 768), up_out=(896, 1024), dense_in=(1920, 256), down_in=(2176, 1024),
             joined_in=(3200, 2048), up_in=(5248, 2048), dense_out=(7296, 2048), down_out=(9344, 2048))
TRADED = 3200
PICKED = 11392


def remote(src, dst, sems, index, device):
    send, recv = sems
    return pltpu.make_async_remote_copy(
        src_ref=src, dst_ref=dst, send_sem=send.at[index], recv_sem=recv.at[index],
        device_id=device, device_id_type=MESH_ID)


def places():
    return tuple(lax.axis_index(a) for a in AXES)


def at_home():
    _, _, c, xh, _ = places()
    return 1 - (xh - c) * (xh - c)


def meet(peers):
    barrier = pltpu.get_barrier_semaphore()
    for p in peers:
        pl.semaphore_signal(barrier, inc=1, device_id=p, device_id_type=MESH_ID)
    pl.semaphore_wait(barrier, len(peers))


def group_peer(n):
    _, _, c, _, z = places()
    return {"c": lax.rem(c + n // 4, 2), "z": lax.rem(z + n % 4, 4)}


def group_peers():
    return [group_peer(n) for n in range(1, 8)]


def diagonal():
    _, _, c, xh, _ = places()
    return {"c": 1 - c, "xh": 1 - xh}


def plane_peers():
    xl, y, c, xh, _ = places()
    peers = []
    for d in range(1, 4):
        for core in (0, 1):
            peers.append({"y": lax.rem(y + d, 4), "c": core})
            x = lax.rem(xh * 2 + xl + d, 4)
            peers.append({"xh": x // 2, "xl": lax.rem(x, 2), "c": core})
    return peers


def block(ref, n, size=128):
    return ref.at[pl.ds(pl.multiple_of(n * size, size), size)]


def loop(count, body, first=0):
    def run(i, carry):
        body(i)
        return carry

    lax.fori_loop(first, count, run, 0)


class GroupGather:
    SEMS = [DMA((8, 4)), DMA((8, 4))]

    def __init__(self, dst, send, recv):
        self.dst, self.sems = dst, (send, recv)
        _, _, self.c, _, self.z = places()
        self.up, self.down, self.other = group_peer(1), group_peer(3), group_peer(4)

    def at(self, core, z, j):
        return self.dst.at[pl.ds(pl.multiple_of((core * 4 + z) * 128 + j * 32, 32), 32)]

    def copy(self, z, j, kind, device):
        ref = self.at(self.c, z, j)
        return remote(ref, ref, self.sems, (kind, j), device)

    def put(self, j):
        self.copy(self.z, j, 0, self.up).start()
        self.copy(self.z, j, 1, self.down).start()
        self.copy(self.z, j, 2, self.other).start()

    def near(self, j):
        below, above = lax.rem(self.z + 3, 4), lax.rem(self.z + 1, 4)
        self.copy(below, j, 0, self.up).wait_recv()
        if j < 2:
            self.copy(below, j, 3, self.up).start()
        self.copy(below, j, 5, self.other).start()
        self.copy(above, j, 1, self.down).wait_recv()
        if j >= 2:
            self.copy(above, j, 4, self.down).start()
        self.copy(above, j, 6, self.other).start()

    def far(self, j):
        opposite = lax.rem(self.z + 2, 4)
        self.copy(opposite, j, 3 if j < 2 else 4, self.up).wait_recv()
        self.copy(opposite, j, 7, self.other).start()

    def shared(self, kind):
        loop(4, lambda j: self.copy(self.z, j, kind, self.other).wait_recv())

    def finish(self):
        def end(j):
            for kind in (0, 1, 2, 3 + j // 2, 5, 6, 7):
                self.copy(self.z, j, kind, self.other).wait_send()

        loop(4, end)


class LowGather:
    SEMS = [DMA((8,)), DMA((8,))]

    def __init__(self, dst, send, recv):
        self.dst, self.sems = dst, (send, recv)
        _, _, c, _, z = places()
        self.own = pl.ds(pl.multiple_of((c * 4 + z) * 128, 128), 128)

    def copy(self, n):
        ref = self.dst.at[:, self.own]
        return remote(ref, ref, self.sems, (n,), group_peer(n))

    def start(self, value):
        self.dst[:, self.own] = value
        loop(8, lambda n: self.copy(n).start(), 1)

    def wait(self):
        loop(8, lambda n: self.copy(n).wait(), 1)


class LowSum:
    SEMS = [DMA((8,)), DMA((8,))]

    def __init__(self, src, got, send, recv):
        self.src, self.got, self.sems = src, got, (send, recv)
        _, _, self.c, _, self.z = places()

    def copy(self, n):
        p = group_peer(n)
        cols = pl.ds(pl.multiple_of((p["c"] * 4 + p["z"]) * 128, 128), 128)
        return remote(self.src.at[:, cols], self.got.at[n], self.sems, (n,), p)

    def start(self):
        loop(8, lambda n: self.copy(n).start(), 1)

    def total(self):
        loop(8, lambda n: self.copy(n).wait(), 1)
        own = pl.ds(pl.multiple_of((self.c * 4 + self.z) * 128, 128), 128)
        out = self.src[:, own].astype(F32)
        for n in range(1, 8):
            out = out + self.got[n].astype(F32)
        return out.astype(BF16)


class PlaneGather:
    SEMS = [DMA((1,)), DMA((41,)), DMA((16, 2))]

    def __init__(self, src, dst, by_rows, local_sem, send, recv):
        self.src, self.dst, self.by_rows, self.local_sem, self.sems = src, dst, by_rows, local_sem, (send, recv)
        self.xl, self.y, self.c, self.xh, _ = places()
        self.x = self.xh * 2 + self.xl
        self.home = at_home()
        r = lax.rem(self.x - 2 * self.c + 4, 4)
        self.odd = 1 - lax.rem(r, 2)
        self.even = lax.rem(r, 2)
        self.away = lax.rem(r - self.odd + 4, 4)

    def whole(self, xl, y, core):
        k = (xl * 4 + y) * 2 + core
        if self.by_rows:
            return block(self.dst, k)
        return self.dst.at[:, pl.ds(pl.multiple_of(k * 128, 128), 128)]

    def half(self, ref, h):
        n = ref.shape[0] // 2
        return ref.at[pl.ds(pl.multiple_of(h * n, n), n)]

    def copy(self, place, h, n, device, src=None):
        xl, y, core = place
        send, recv = self.sems
        dst = self.half(self.whole(*place), h)
        return pltpu.make_async_remote_copy(
            src_ref=dst if src is None else self.half(src, h), dst_ref=dst, send_sem=send.at[n],
            recv_sem=recv.at[(xl * 4 + y) * 2 + core, h], device_id=device, device_id_type=MESH_ID)

    def arrived(self, place, h):
        self.copy(place, h, 0, {"c": 1 - self.c}).wait_recv()

    def arrived_whole(self, place):
        loop(2, lambda h: self.arrived(place, h))

    def chip(self, dx, dy, core):
        x = lax.rem(self.x + dx, 4)
        return {"xh": x // 2, "xl": lax.rem(x, 2), "y": lax.rem(self.y + dy, 4), "c": core}

    def both_ways(self, place, n, along_x, along_y, core, src=None):
        def send(i):
            d = 1 + 2 * lax.rem(i, 2)
            h = lax.rem(i + i // 2, 2)
            self.copy(place, h, n + i, self.chip(along_x * d, along_y * d, core), src).start()

        loop(4, send)

    def local(self):
        return pltpu.make_async_copy(self.src, self.whole(self.xl, self.y, self.c), self.local_sem.at[0])

    def start(self):
        place = (self.xl, self.y, self.c)

        @pl.when(self.home == 1)
        def _():
            self.local().start()

        self.both_ways(place, 0, 1 - self.c, self.c, self.xh, self.src)

        @pl.when(self.home == 0)
        def _():
            loop(2, lambda h: self.copy(place, h, 39 + h, {"c": 1 - self.c}, self.src).start())

    def row(self, d):
        return lax.rem(self.y + d, 4)

    def along_y(self, e):
        self.both_ways((e, self.y, 0), 4 + 4 * e, 0, 1, self.c)

    def along_x(self, d):
        self.both_ways((self.xl, self.row(d), 1), 23 + 4 * d, 1, 0, self.c)

    def step(self, n):
        if n == 0:
            @pl.when(self.home == 1)
            def _():
                self.local().wait()
                self.arrived_whole((self.xl, self.y, 1 - self.c))
                self.along_y(self.xl)
                self.along_x(0)
        elif n == 1:
            place, h = (self.odd, self.y, 0), self.away // 2
            self.arrived(place, h)
            self.copy(place, h, 12, self.chip(self.away, 0, self.c)).start()

            @pl.when(self.home == 1)
            def _():
                def pass_y(k):
                    place = (self.xl, self.row(3 - 2 * k), 1)
                    self.arrived(place, k)
                    self.copy(place, k, 21 + k, self.chip(0, 1 + 2 * k, self.c)).start()

                loop(2, pass_y)
        elif n == 2:
            self.arrived((self.odd, self.y, 0), 1 - self.away // 2)
            self.along_y(self.odd)

            @pl.when(self.home == 1)
            def _():
                def spread(k):
                    self.arrived((self.xl, self.row(3 - 2 * k), 1), 1 - k)
                    self.along_x(3 - 2 * k)

                loop(2, spread)
        elif n == 3:
            @pl.when(self.home == 0)
            def _():
                self.arrived_whole((self.even, self.y, 0))
                self.along_y(self.even)

            @pl.when(self.home == 1)
            def _():
                self.arrived_whole((self.xl, self.row(2), 1))
                self.along_x(2)
        elif n == 4:
            def pass_on(i):
                e, k = i // 2, lax.rem(i, 2)
                place = (e, self.row(3 - 2 * k), 0)
                self.arrived(place, k)
                self.copy(place, k, 13 + i, self.chip(0, 1 + 2 * k, self.c)).start()

            loop(4, pass_on)
        else:
            def pass_on(i):
                k = i * (3 if n == 5 else 1) + (n - 5)
                place, h = (self.odd, self.row(k), 1), self.away // 2
                self.arrived(place, h)
                self.copy(place, h, 17 + k, self.chip(self.away, 0, self.c)).start()

            loop(2, pass_on)

    def wait(self):
        def rows(e):
            loop(2, lambda k: self.arrived((e, self.row(3 - 2 * k), 0), 1 - k))
            self.arrived_whole((e, self.row(2), 0))

        loop(2, rows)
        loop(4, lambda y: self.arrived((self.odd, y, 1), 1 - self.away // 2))

        @pl.when(self.home == 0)
        def _():
            loop(4, lambda y: self.arrived_whole((self.even, y, 1)))

    def finish(self):
        sent = lambda n: self.copy((0, 0, 0), 0, n, {"c": 1 - self.c}).wait_send()
        loop(21, sent)

        @pl.when(self.home == 1)
        def _():
            loop(39, sent, 21)

        @pl.when(self.home == 0)
        def _():
            loop(41, sent, 39)


class GroupSum:
    NAMES = ("far_up", "far_down", "up_high", "down_low", "up_low", "down_high")
    SCRATCH = [VMEM((1024, 2048), BF16), VMEM((4, 128, 2048), BF16), VMEM((3, 128, 2048), BF16),
               VMEM((2, 64, 2048), BF16), VMEM((2, 128, 2048), BF16), DMA((10,)), DMA((10,))]

    def __init__(self, parts, near, sent, half, full, send, recv):
        self.parts, self.near, self.sent, self.half, self.full, self.sems = parts, near, sent, half, full, (send, recv)
        _, _, self.c, _, self.z = places()
        self.up, self.down, self.other = group_peer(1), group_peer(3), group_peer(4)
        self.order = [lax.rem(self.z + d, 4) for d in (2, 1, 3, 0)]

    def part(self, core, i):
        return block(self.parts, core * 4 + self.order[i])

    def given(self, i):
        return remote(self.part(1 - self.c, i), self.near.at[i], self.sems, (i,), self.other)

    def give_from(self, i, at):
        remote(block(self.parts, (1 - self.c) * 4 + at), self.near.at[i], self.sems, (i,), self.other).start()

    def give(self, i):
        self.given(i).start()

    def pair(self, i, rows=slice(None)):
        return self.part(self.c, i)[rows].astype(F32) + self.near[i, rows].astype(F32)

    def piece(self, name):
        low, high = pl.ds(0, 64), pl.ds(64, 64)
        n = self.NAMES.index(name)
        src = (self.sent.at[0, low], self.sent.at[0, high], self.sent.at[1, high], self.sent.at[2, low],
               self.sent.at[1, low], self.sent.at[2, high])[n]
        dst = (self.half.at[0], self.half.at[1], self.full.at[0, high], self.full.at[1, low],
               self.full.at[0, low], self.full.at[1, high])[n]
        return remote(src, dst, self.sems, (4 + n,), (self.up, self.down)[n % 2])

    def far(self):
        self.given(0).wait_recv()
        self.sent[0] = self.pair(0).astype(BF16)
        self.piece("far_up").start()
        self.piece("far_down").start()

    def near_up(self):
        self.given(1).wait_recv()
        self.sent[1, pl.ds(64, 64)] = self.pair(1, pl.ds(64, 64)).astype(BF16)
        self.piece("up_high").start()

    def near_down(self):
        self.given(2).wait_recv()
        self.sent[2, pl.ds(0, 64)] = self.pair(2, pl.ds(0, 64)).astype(BF16)
        self.piece("down_low").start()

    def pass_on(self):
        low, high = pl.ds(0, 64), pl.ds(64, 64)
        self.piece("far_up").wait_recv()
        self.sent[1, low] = (self.pair(1, low) + self.half[0].astype(F32)).astype(BF16)
        self.piece("up_low").start()
        self.piece("far_down").wait_recv()
        self.sent[2, high] = (self.pair(2, high) + self.half[1].astype(F32)).astype(BF16)
        self.piece("down_high").start()

    def arrive(self):
        self.given(3).wait_recv()
        for name in ("up_high", "down_low", "up_low", "down_high"):
            self.piece(name).wait_recv()

    def total(self, rows=slice(None)):
        return self.pair(3, rows) + self.full[0, rows].astype(F32) + self.full[1, rows].astype(F32)

    def finish(self):
        for name in self.NAMES:
            self.piece(name).wait_send()
        for i in range(4):
            self.given(i).wait_send()


def params(cid, mib):
    return pltpu.CompilerParams(collective_id=cid, has_side_effects=True, vmem_limit_bytes=mib << 20)


def plain(mib):
    return pltpu.CompilerParams(vmem_limit_bytes=mib << 20)


def shape(*dims, dtype=BF16):
    return jax.ShapeDtypeStruct(dims, dtype)


def specs(*spaces):
    return [pl.BlockSpec(memory_space=s) for s in spaces]


def layer_norm(rows_in, gain, shift):
    row_mean = jnp.mean(rows_in, axis=-1, keepdims=True)
    centered = rows_in - row_mean
    variance = jnp.mean(centered * centered, axis=-1, keepdims=True)
    return centered * lax.rsqrt(variance + EPSILON) * gain + shift


def norm_back(rows_in, gain, grad):
    row_mean = jnp.mean(rows_in, axis=-1, keepdims=True)
    centered = rows_in - row_mean
    inverse = lax.rsqrt(jnp.mean(centered * centered, axis=-1, keepdims=True) + EPSILON)
    n = centered * inverse
    e = gain * grad
    return (e - jnp.mean(e, axis=-1, keepdims=True) - n * jnp.mean(e * n, axis=-1, keepdims=True)) * inverse


def dot(a, b, dims=((1,), (0,))):
    return lax.dot_general(a, b, (dims, ((), ())), preferred_element_type=F32)


def dot_t(a, b):
    return dot(a, b, ((1,), (1,)))


def dot_o(a, b):
    return dot(a, b, ((0,), (0,)))


def tiles(count, size, body):
    def run(i, carry):
        body(pl.ds(pl.multiple_of(i * size, size), size))
        return carry

    lax.fori_loop(0, count, run, 0)


def split_refs(refs, *counts):
    refs, out = list(refs), []
    for n in counts:
        out.append(refs[:n])
        refs = refs[n:]
    return (*out, refs)


def pick(ref, name):
    first, n = PICKS[name]
    return ref[:, pl.ds(first, n)]


def row_pair(z):
    return (pl.ds(pl.multiple_of(z * 128, 128), 128), pl.ds(pl.multiple_of(512 + z * 128, 128), 128))


def take_pair(ref, z, cols=slice(None)):
    a, b = row_pair(z)
    return jnp.concatenate([ref[a, cols], ref[b, cols]], axis=0)


def put_pair(ref, z, value, cols=slice(None)):
    a, b = row_pair(z)
    ref[a, cols] = value[:128]
    ref[b, cols] = value[128:]


class Swap:
    def __init__(self, pairs, local, send, recv):
        self.pairs, self.local, self.sems, self.home = pairs, local, (send, recv), at_home()

    def near_copy(self, n):
        src, _, dst = self.pairs[n]
        return pltpu.make_async_copy(src, dst, self.local.at[n])

    def far_copy(self, n):
        src, dst, _ = self.pairs[n]
        return remote(src, dst, self.sems, (n,), diagonal())

    def start(self, n):
        @pl.when(self.home == 1)
        def _():
            self.near_copy(n).start()

        @pl.when(self.home == 0)
        def _():
            self.far_copy(n).start()

    def wait(self, n):
        @pl.when(self.home == 1)
        def _():
            self.near_copy(n).wait()

        @pl.when(self.home == 0)
        def _():
            self.far_copy(n).wait_recv()

    def finish(self):
        @pl.when(self.home == 0)
        def _():
            for n in range(len(self.pairs)):
                self.far_copy(n).wait_send()

    @staticmethod
    def sems(n):
        return [DMA((n,)), DMA((n,)), DMA((n,))]


class Spread:
    SCRATCH = [VMEM((16, 5, 8, 128), BF16), VMEM((16, 5, 8, 128), BF16), VMEM((8, 3, 8, 128), BF16),
               VMEM((8, 8, 128), BF16), DMA((16,)), DMA((16,)), DMA((9,)), DMA((16,)), DMA((20,)), DMA((20,)), DMA((2,))]

    def __init__(self, split, whole, send, got, part, full, one_send, one_recv, two_send, two_recv, send3, recv3, local):
        self.split, self.whole, self.send, self.got, self.part, self.full = split, whole, send, got, part, full
        self.one, self.two, self.three, self.local = (one_send, one_recv), (two_send, two_recv), (send3, recv3), local
        self.xl, self.y, self.c, self.xh, self.z = places()
        self.q = (self.xh * 2 + self.xl) * 4 + self.y
        self.home = at_home()

    def put(self, n, value):
        for m in range(4):
            k = 2 * n + m
            where = (k // 3, k % 3) if k < 48 else (k - 48, 3)
            row, col = m % 2 * 8, m // 2 * 128
            self.send[where] = value[row:row + 8, col:col + 128].astype(BF16)

    def mark(self, hot):
        for j in range(16):
            self.send[j, 4] = hot

    def chip(self, n):
        q = lax.rem(self.q + n, 16)
        x = q // 4
        return q, {"xh": x // 2, "xl": lax.rem(x, 2), "y": lax.rem(q, 4)}

    def to_owner(self, n):
        q, device = self.chip(n)
        return remote(self.send.at[q], self.got.at[n], self.one, (n,), device)

    def start(self):
        loop(16, lambda n: self.to_owner(n).start(), 1)

    def add(self):
        self.got[0] = self.send[self.q]
        loop(16, lambda n: self.to_owner(n).wait_recv(), 1)
        for b in range(8):
            def more(n, total, b=b):
                return total + self.got[n, 0:4].astype(F32) * self.got[n, 4].astype(F32)[b:b + 1]

            total = lax.fori_loop(0, 16, more, jnp.zeros((4, 8, 128), F32)).astype(BF16)
            self.part[b] = total[:3]
            self.full[b] = total[3]

    def copy_to_groups(self, slot, i):
        device = {"xh": self.c, "xl": lax.rem(self.xl + i // 4, 2), "y": lax.rem(self.y + lax.rem(i, 4), 4)}
        send, recv = self.two
        return pltpu.make_async_remote_copy(
            src_ref=self.part, dst_ref=self.split.at[:, slot], send_sem=send.at[i],
            recv_sem=recv.at[self.q], device_id=device, device_id_type=MESH_ID)

    def split_copy(self, i):
        return self.copy_to_groups(self.q, i)

    def split_own(self):
        return pltpu.make_async_copy(self.part, self.split.at[:, self.q], self.local.at[0])

    def whole_own(self):
        return pltpu.make_async_copy(self.full, self.whole.at[:, self.c * 4 + self.z, self.q], self.local.at[1])

    def line_copies(self):
        where = self.whole.at[:, self.c * 4 + self.z, self.q]
        return [remote(self.full, where, self.three, (d,), {"z": lax.rem(self.z + d, 4)}) for d in (1, 2, 3)]

    def plane_copy(self, n):
        where = self.whole.at[:, pl.ds(self.c * 4, 4), self.q]
        return remote(where, where, self.three, (4 + n,), self.chip(n)[1])

    def shared_whole(self):
        where = self.whole.at[:, pl.ds(self.c * 4, 4)]
        return remote(where, where, self.three, (0,), {"c": 1 - self.c})

    def shared_split(self):
        send, recv = self.two
        return pltpu.make_async_remote_copy(
            src_ref=self.split, dst_ref=self.split, send_sem=send.at[8], recv_sem=recv.at[0],
            device_id={"c": 1 - self.c}, device_id_type=MESH_ID)

    def deal_groups(self):
        @pl.when(self.home == 1)
        def _():
            self.split_own().start()

        @pl.when(self.home == 0)
        def _():
            self.split_copy(0).start()

        loop(8, lambda i: self.split_copy(i).start(), 1)

    def deal(self):
        self.whole_own().start()
        for copy in self.line_copies():
            copy.start()
        self.deal_groups()

    def deal_plane(self):
        self.whole_own().wait()
        for copy in self.line_copies():
            copy.wait_recv()
        loop(16, lambda n: self.plane_copy(n).start(), 1)

    def wait_groups(self, count):
        send, recv = self.two
        def wait(q):
            @pl.when(self.q != q)
            def _():
                pltpu.make_async_remote_copy(
                    src_ref=self.part, dst_ref=self.split.at[:, q], send_sem=send.at[0], recv_sem=recv.at[q],
                    device_id={"c": 1 - self.c}, device_id_type=MESH_ID).wait_recv()

        loop(count, wait)

    def share(self):
        @pl.when(self.home == 1)
        def _():
            self.split_own().wait()
            self.wait_groups(16)
            self.shared_split().start()

        loop(16, lambda n: self.plane_copy(n).wait_recv(), 1)
        self.shared_whole().start()

    def finish_shares(self):
        self.shared_whole().wait()

        @pl.when(self.home == 1)
        def _():
            self.shared_split().wait_send()

        @pl.when(self.home == 0)
        def _():
            self.shared_split().wait_recv()

    def finish_groups(self):
        @pl.when(self.home == 0)
        def _():
            self.split_copy(0).wait_send()

        loop(8, lambda i: self.split_copy(i).wait_send(), 1)

    def finish(self):
        self.finish_shares()
        self.finish_groups()
        for copy in self.line_copies():
            copy.wait_send()

        def end(n):
            self.plane_copy(n).wait_send()
            self.to_owner(n).wait_send()

        loop(16, end, 1)


class LastSpread(Spread):
    SCRATCH = [VMEM((16, 2, 8, 128), BF16), VMEM((16, 2, 8, 128), BF16), VMEM((8, 8, 128), BF16),
               DMA((16,)), DMA((16,)), DMA((9,)), DMA((16,)), DMA((20,)), DMA((20,)), DMA((2,))]

    def __init__(self, split, whole, send, got, part, *sems):
        super().__init__(split, whole, send, got, part, part, *sems)

    def put(self, n, value):
        for m in range(4):
            row, col = m % 2 * 8, m // 2 * 128
            self.send[2 * n + m, 0] = value[row:row + 8, col:col + 128].astype(BF16)

    def mark(self, hot):
        for j in range(16):
            self.send[j, 1] = hot

    def add(self):
        self.got[0] = self.send[self.q]
        loop(16, lambda n: self.to_owner(n).wait_recv(), 1)
        for b in range(8):
            def more(n, total, b=b):
                return total + self.got[n, 0].astype(F32) * self.got[n, 1].astype(F32)[b:b + 1]

            self.part[b] = lax.fori_loop(0, 16, more, jnp.zeros((8, 128), F32)).astype(BF16)

    def split_copy(self, i):
        return self.copy_to_groups(lax.rem(self.q, 12), i)

    def split_own(self):
        return pltpu.make_async_copy(self.part, self.split.at[:, lax.rem(self.q, 12)], self.local.at[0])

    def late(self):
        return lax.rem(self.q, 4)

    def whole_own(self):
        return pltpu.make_async_copy(self.part, self.whole.at[:, self.c * 4 + self.z, self.late()], self.local.at[1])

    def line_copies(self):
        where = self.whole.at[:, self.c * 4 + self.z]
        return [remote(where, where, self.three, (d,), {"z": lax.rem(self.z + d, 4)}) for d in (1, 2, 3)]

    def plane_copy(self, n):
        where = self.whole.at[:, self.c * 4 + self.z, self.late()]
        return remote(self.part, where, self.three, (4 + n,), self.chip(n)[1])

    def deal(self):
        @pl.when(self.q >= 12)
        def _():
            self.whole_own().start()
            loop(16, lambda n: self.plane_copy(n).start(), 1)

        @pl.when(self.q < 12)
        def _():
            self.deal_groups()

    def share_groups(self):
        @pl.when(self.home == 1)
        def _():
            @pl.when(self.q < 12)
            def _():
                self.split_own().wait()

            self.wait_groups(12)
            self.shared_split().start()

    def line(self):
        @pl.when(self.q >= 12)
        def _():
            self.whole_own().wait()

        def late(n):
            @pl.when(lax.rem(self.q - n + 16, 16) >= 12)
            def _():
                self.plane_copy(n).wait_recv()

        loop(16, late, 1)

        for copy in self.line_copies():
            copy.start()

    def share_line(self):
        for copy in self.line_copies():
            copy.wait_recv()
        self.shared_whole().start()

    def finish(self):
        self.finish_shares()

        @pl.when(self.q < 12)
        def _():
            self.finish_groups()

        @pl.when(self.q >= 12)
        def _():
            loop(16, lambda n: self.plane_copy(n).wait_send(), 1)

        for copy in self.line_copies():
            copy.wait_send()
        loop(16, lambda n: self.to_owner(n).wait_send(), 1)


def far_peers():
    xl, y, _, xh, _ = places()
    peers = []
    for d in range(1, 4):
        x = lax.rem(xh * 2 + xl + d, 4)
        for e in range(1, 4):
            peers.append({"xh": x // 2, "xl": lax.rem(x, 2), "y": lax.rem(y + e, 4)})
    return peers


ROOT_HALF = 0.7071067811865476
ROOT_TAU = 0.3989422804014327
SETS = dict(joined_in=(0, 0), up_in=(128, 0), dense_out=(256, 0), down_out=(384, 0), up_out=(512, 0),
            down_in=(512, 1024), joined_out=(640, 0), dense_in=(640, 768))


def cast_parts(value):
    high = value.astype(BF16).astype(F32)
    middle = (value - high).astype(BF16).astype(F32)
    return high, middle, value - high - middle


def block_kernel(*refs):
    (ids, tokens, go, *vectors), adapters, shards, outs, scratch = split_refs(refs, 11, 8, 4, 6)
    back, out, split, whole, split2, whole2 = outs
    names = list(SCRATCH)
    v = dict(zip(names, scratch))
    rest = list(scratch[len(names):])

    def sems(n):
        taken = rest[:n]
        del rest[:n]
        return taken

    load_sem, vector_sem, copy_sem = sems(3)
    xl, y, c, xh, z = places()
    own = c * 4 + z
    mine_rows = pl.ds(pl.multiple_of(own * 128, 128), 128)
    there_rows = (1 - c) * 4 + z
    gain1, shift1, gain2, shift2, bias_d, bias_n = (v["lines"].at[n:n + 1] for n in range(6))
    pk, xs, xbuf, gbuf = v["pk"], v["xs"], v["xbuf"], v["gbuf"]
    sets = v["parts"]
    loads = {}
    for n, (name, ref) in enumerate(zip(SETS, adapters)):
        row, col = SETS[name]
        loads[name] = pltpu.make_async_copy(ref, sets.at[pl.ds(row, 128), pl.ds(col, ref.shape[1])], load_sem.at[n])
        loads[name].start()
    lines = [pltpu.make_async_copy(ref, v["lines"].at[n:n + 1], vector_sem.at[n]) for n, ref in enumerate(vectors[:6])]
    for line in lines:
        line.start()
    meet(plane_peers() + group_peers() + far_peers())

    bias = v["bias"]
    mine = v["mine"]
    piece = lambda who, j: gbuf.at[pl.ds(pl.multiple_of(who * 128 + j * 32, 32), 32)]
    sub = lambda ref, j: ref.at[pl.ds(j * 32, 32)]
    pairs = [(sub(tokens, j), sub(xs, j), sub(xs, j)) for j in range(4)]
    pairs += [(m, p, p) for m, p in ((mine, pk.at[:, :TRADED]), (vectors[7], v["bias_one"]), (vectors[6], bias))]
    pairs += [(sub(go, j), piece(there_rows, j), piece(own, j)) for j in range(4)]
    sw = Swap(pairs, *sems(3))
    for j in ORDER:
        sw.start(j)
    joined = PlaneGather(shards[0], v["wj"], True, *sems(3))
    dense = PlaneGather(shards[1], v["wd"], False, *sems(3))
    down = PlaneGather(shards[2], v["wn"], False, *sems(3))
    up = PlaneGather(shards[3], v["wu"], True, *sems(3))
    joined.start()
    set_id = ids[0]
    for name in ("joined_out", "up_out", "dense_in", "down_in"):
        (row, col), (first, n) = SETS[name], PICKS[name]
        loads[name].wait()
        chosen = sets[row:row + 16, col:col + n]
        for k in range(1, 8):
            chosen = jnp.where(set_id == k, sets[row + k * 16:row + k * 16 + 16, col:col + n], chosen)
        mine[:, first:first + n] = chosen
    first, n = PICKS["hot"]
    mine[:, first:first + n] = jnp.where(lax.broadcasted_iota(jnp.int32, (16, 128), 0) == set_id, 1.0, 0.0).astype(BF16)
    for n in (4, 5, 6):
        sw.start(n)
    for line in lines:
        line.wait()
    g1 = GroupGather(xbuf, *sems(2))
    for j in ORDER:
        sw.wait(j)
        x1 = layer_norm(xs[j * 32:(j + 1) * 32].astype(F32), gain1[...], shift1[...])
        xbuf[pl.ds(pl.multiple_of(own * 128 + j * 32, 32), 32)] = x1.astype(BF16)
        g1.put(j)
    dense.start()
    joined.step(0)
    joined.step(1)
    g1.near(0)
    joined.step(2)
    g1.near(3)
    joined.step(3)
    g1.near(1)
    joined.step(4)
    g1.near(2)
    joined.step(5)
    joined.step(6)
    for j in ORDER:
        sw.start(7 + j)
    dense.step(0)
    dense.step(1)
    down.start()
    sw.wait(4)
    for name in ("joined_in", "up_in", "dense_out", "down_out"):
        (row, col), (first, n) = SETS[name], PICKS[name]
        loads[name].wait()
        chosen = jnp.zeros((16, n), F32)
        for k in range(8):
            chosen = chosen + sets[row + k * 16:row + k * 16 + 16, col:col + n].astype(F32) * pk[k:k + 1, 0:1].astype(F32)
        pk[:, first:first + n] = chosen.astype(BF16)

    def low_pair(at):
        low = dot_t(pick(pk, "joined_in"), take_pair(xbuf, at)).astype(BF16)
        for n, rows in enumerate(row_pair(at)):
            v["low_q"][:, rows] = low[:, n * 128:n * 128 + 128]

    g1.shared(2)
    low_pair(z)
    for j in ORDER:
        g1.far(j)
    g1.shared(5)
    low_pair(lax.rem(z + 3, 4))
    g1.shared(6)
    low_pair(lax.rem(z + 1, 4))
    g1.shared(7)
    low_pair(lax.rem(z + 2, 4))
    g2 = GroupGather(gbuf, *sems(2))
    for n in (5, 6):
        sw.wait(n)
    joined.wait()

    lane = lax.broadcasted_iota(jnp.int32, (256, 128), 1)
    row = lax.broadcasted_iota(jnp.int32, (256, 128), 0)
    qa, ka, va = v["qa"], v["ka"], v["va"]

    def project(i, carry):
        rows = pl.ds(pl.multiple_of(i * 256, 256), 256)
        acc = dot(xbuf[rows], v["wj"][...]) + dot_o(v["low_q"][:, rows], pick(pk, "joined_out")) + v["bias_one"][...].reshape(1, 768)
        b = acc.astype(BF16).astype(F32)
        position = (i * 256 + row).astype(F32) * 0.125
        ones = jnp.where(lane < 67, 1.0, 0.0)
        for h in range(4):
            slope = jnp.exp2((own * 4 + h + 1).astype(F32) * (-8.0 / HEADS) + jnp.zeros((1, 128), F32))
            high, middle, lowest = cast_parts(position * slope)
            tail = jnp.where(lane == 64, high, jnp.where(lane == 65, middle, jnp.where(lane == 66, lowest, jnp.where(
                lane < 70, 1.0, 0.0))))
            at = h * 192
            qa[h, rows] = jnp.where(lane < 64, b[:, at:at + 128] * 0.125, ones).astype(BF16)
            ka[h, rows] = jnp.where(lane < 64, b[:, at + 64:at + 192], tail).astype(BF16)
            value = jnp.concatenate([b[:, at + 128:at + 192], b[:, at:at + 64]], axis=1)
            va[h, rows] = jnp.where(lane < 64, value, ones).astype(BF16)
        return carry

    lax.fori_loop(0, 4, project, 0)
    own_cols = pl.ds(pl.multiple_of(own * 256, 256), 256)
    keep = lambda n, ref: pltpu.make_async_copy(ref.at[:, own_cols], v["cols"].at[n], copy_sem.at[n])
    keep(0, xbuf).start()
    for j in ORDER:
        sw.wait(7 + j)
        g2.put(j)

    hooks = [lambda: dense.step(2), lambda: down.step(0), lambda: (dense.step(3), down.step(1)), lambda: g2.near(0), lambda: dense.step(4),
             lambda: g2.near(3), lambda: down.step(2), lambda: g2.near(1), lambda: (dense.step(5), dense.step(6)),
             lambda: g2.near(2), lambda: up.start(), lambda: down.step(3), lambda: (g2.far(0), g2.far(3)),
             lambda: None, lambda: (g2.far(1), g2.far(2)), lambda: down.step(4)]
    mask = lax.broadcasted_iota(jnp.int32, (256, 256), 0) <= lax.broadcasted_iota(jnp.int32, (256, 256), 1)
    line = lax.broadcasted_iota(jnp.int32, (128, 256), 0)
    c4 = v["c4"]

    def head(h, carry):
        for i in range(4):
            rows = pl.ds(i * 256, 256)
            q = qa[h, rows]
            last = jnp.where(mask, dot_t(ka[h, rows], q), MASKED)
            top = jnp.max(last, axis=0, keepdims=True)
            if i:
                before = dot_t(ka[h, pl.ds(0, i * 256)], q)
                top = jnp.maximum(top, jnp.max(before, axis=0, keepdims=True))
            mix = dot_o(va[h, rows], jnp.exp(last - top).astype(BF16))
            if i:
                mix = mix + dot_o(va[h, pl.ds(0, i * 256)], jnp.exp(before - top).astype(BF16))
            total = mix[64:65]
            high, middle, lowest = cast_parts(-(top + jnp.log(total)))
            mix = jnp.where(line == 67, high, jnp.where(line == 68, middle, jnp.where(
                line == 69, lowest, mix / total)))
            turned = mix.T
            c4[h, rows] = turned.astype(BF16)
            qa[h, rows] = jnp.where(lane < 67, q.astype(F32), jnp.where(lane < 70, turned, 0.0)).astype(BF16)
            for k in range(4):
                @pl.when(h == k)
                def _(k=k, i=i):
                    hooks[k * 4 + i]()
        return carry

    lax.fori_loop(0, 4, head, 0)
    ctx = v["ctx"]
    for h in (0, 2):
        ctx[:, h * 64:h * 64 + 128] = jnp.concatenate([c4[h, :, :64], c4[h + 1, :, :64]], axis=1)

    v["gos"][...] = gbuf[mine_rows]

    src, got = v["low_src"], v["low_got"]
    src[0] = dot_t(pick(pk, "dense_in"), ctx[...]).astype(BF16)
    sum_d = LowSum(src.at[0], got.at[0], *sems(2))
    sum_d.start()
    s1 = GroupSum(*[v[n] for n in ("parts", "near", "sent", "half", "full")], *sems(2))
    dense.wait()
    keep(0, xbuf).wait()
    g1.finish()

    def summed(s, compute, before=lambda: None, beside=lambda: None):
        def part(i, carry):
            compute(s, lax.rem(z + 2 - i + 3 * (i // 2) - 2 * (i // 3) + 4, 4))
            s.give_from(i, lax.rem(z + 2 - i + 3 * (i // 2) - 2 * (i // 3) + 4, 4))

            @pl.when(i == 1)
            def _():
                before()
                s.far()

            @pl.when(i == 2)
            def _():
                s.near_up()

            return carry

        lax.fori_loop(0, 4, part, 0)
        s.near_down()
        beside()
        s.pass_on()

    def dense_part(s, at):
        put_pair(s.parts, at, dot(take_pair(ctx, at), v["wd"][...]).astype(BF16))

    def low_tile(rows):
        v["low_g"][:, rows] = dot_t(pick(pk, "down_out"), gbuf[rows]).astype(BF16)

    def beside_dense():
        for kind in (2, 5, 6, 7):
            g2.shared(kind)
        keep(3, gbuf).start()
        down.step(5)
        up.step(0)
        tiles(4, 256, low_tile)
        down.step(6)
        up.step(1)

    summed(s1, dense_part, beside=beside_dense)
    up.step(2)
    mid, dmid, dact = v["mid"], v["dmid"], v["dact"]
    total_d = sum_d.total()
    mid[...] = dot_o(total_d, pick(pk, "dense_out")) + bias_d[...] + xs[...].astype(F32)
    down.wait()

    def grad_act(rows):
        dact[rows] = dot_t(gbuf[rows], v["wn"][...]) + dot_o(v["low_g"][:, rows], pick(pk, "down_in"))

    def grad_acts(i, carry):
        grad_act(pl.ds(pl.multiple_of(i * 256, 256), 256))

        @pl.when(i == 1)
        def _():
            up.step(3)

        return carry

    lax.fori_loop(0, 4, grad_acts, 0)
    up.step(4)
    s1.arrive()
    g3 = GroupGather(xbuf, *sems(2))
    for j in ORDER:
        rows = slice(j * 32, (j + 1) * 32)
        mid[rows] = mid[rows] + s1.total(rows)
        xbuf[pl.ds(pl.multiple_of(own * 128 + j * 32, 32), 32)] = layer_norm(mid[rows], gain2[...], shift2[...]).astype(BF16)
        g3.put(j)
    all_d = LowGather(v["sum_d"], *sems(2))
    all_d.start(total_d)
    up.step(5)
    up.step(6)
    up.wait()
    act, dpre = v["act"], v["dpre"]

    def forward(at):
        x = take_pair(xbuf, at)
        lu = dot_t(pick(pk, "up_in"), x).astype(BF16)
        for n, rows in enumerate(row_pair(at)):
            v["low_u"][:, rows] = lu[:, n * 128:n * 128 + 128]

        def run(n, carry):
            cols = pl.ds(pl.multiple_of(n * 256, 256), 256)
            w = pk[:, pl.ds(pl.multiple_of(PICKS["up_out"][0] + n * 256, 128), 256)]
            b = bias[:, pl.ds(pl.multiple_of(n * 256, 256), 256)]
            pre = dot(x, v["wu"][:, cols]) + dot_o(lu, w) + b
            cdf = 0.5 * (1.0 + lax.erf(pre * ROOT_HALF))
            put_pair(act, at, (pre * cdf).astype(BF16), cols)
            slope = cdf + pre * (jnp.exp(-0.5 * pre * pre) * ROOT_TAU)
            put_pair(dpre, at, (take_pair(dact, at, cols) * slope).astype(BF16), cols)
            return carry

        lax.fori_loop(0, 4, run, 0)

    def by_pairs(g, work, beside=None):
        def run(p, carry):
            @pl.when(p == 0)
            def _():
                g.shared(2)

            @pl.when(p == 1)
            def _():
                if beside:
                    beside()
                for j in ORDER:
                    g.near(j)
                g.shared(6)

            @pl.when(p == 2)
            def _():
                g.shared(5)

            @pl.when(p == 3)
            def _():
                for j in ORDER:
                    g.far(j)
                g.shared(7)

            work(lax.rem(z + p + p // 2 - 2 * (p // 3), 4))
            return carry

        lax.fori_loop(0, 4, run, 0)

    by_pairs(g3, forward)
    keep(2, xbuf).start()

    sum_u = LowSum(src.at[1], got.at[1], *sems(2))
    s2 = GroupSum(*[v[n] for n in ("parts", "near", "sent", "half", "full")], *sems(2))
    s1.finish()

    def wide(ref, weight):
        def compute(s, at):
            x = take_pair(ref, at)

            def run(n, carry):
                cols = pl.ds(pl.multiple_of(n * 512, 512), 512)
                put_pair(s.parts, at, dot_t(x, weight[cols]).astype(BF16), cols)
                return carry

            lax.fori_loop(0, 4, run, 0)

        return compute

    keep(2, xbuf).wait()
    g3.finish()
    def low_up():
        src[1] = dot_t(pick(pk, "up_out"), dpre[...]).astype(BF16)
        sum_u.start()

    summed(s2, wide(dpre, v["wu"]), beside=low_up)
    for thing in (joined, dense, down, up, sw):
        thing.finish()
    keep(3, gbuf).wait()
    g2.finish()
    mlp = gbuf

    def forward_down(rows):
        mlp[rows] = dot(act[rows], v["wn"][...]).astype(BF16)

    tiles(4, 256, forward_down)
    src[2] = dot_t(pick(pk, "down_in"), act[...]).astype(BF16)
    total_u = sum_u.total()
    dmid[...] = dot_o(total_u, pick(pk, "up_in"))
    sum_n = LowSum(src.at[2], got.at[2], *sems(2))
    sum_n.start()
    all_u = LowGather(v["sum_u"], *sems(2))
    all_u.start(total_u)
    s2.arrive()
    all_n = LowGather(v["sum_n"], *sems(2))
    all_n.start(sum_n.total())
    g4 = GroupGather(xbuf, *sems(2))
    for j in ORDER:
        rows = slice(j * 32, (j + 1) * 32)
        dmid[rows] = v["gos"][rows].astype(F32) + norm_back(mid[rows], gain2[...], dmid[rows] + s2.total(rows))
        xbuf[pl.ds(pl.multiple_of(own * 128 + j * 32, 32), 32)] = dmid[rows].astype(BF16)
        g4.put(j)
    spread = Spread(split, whole, *sems(11))

    def product(first, count, low, ref):
        for n in range(0, count, 2):
            spread.put(first + n, dot(low[...], ref[:, n * 128:n * 128 + 256]))

    def early_products():
        spread.mark(pk[:8, PICKS["hot"][0]:PICKS["hot"][0] + 128])
        product(2, 8, v["low_u"], dpre)
        product(10, 8, v["low_g"], act)
        all_u.wait()
        product(28, 2, v["sum_u"], v["cols"].at[2])

    grads = c4

    def context(at):
        x = take_pair(xbuf, at)
        ld = dot_t(pick(pk, "dense_out"), x).astype(BF16)
        for n, rows in enumerate(row_pair(at)):
            v["low_d"][:, rows] = ld[:, n * 128:n * 128 + 128]
        value = dot_t(x, v["wd"][...]) + dot_o(ld, pick(pk, "dense_in"))
        value = value.astype(BF16).astype(F32)
        mix = take_pair(ctx, at).astype(F32)
        for h in range(4):
            first = h // 2 * 128
            g = value[:, first:first + 128]
            here = (lane // 64) == h % 2
            d = -jnp.sum(jnp.where(here, g * mix[:, first:first + 128], 0.0), axis=-1, keepdims=True)
            high, middle, lowest = cast_parts(d)
            if h % 2:
                g = jnp.concatenate([g[:, 64:], g[:, :64]], axis=1)
            put_pair(grads.at[h], at, jnp.where(lane < 64, g, jnp.where(lane == 64, high, jnp.where(
                lane == 65, middle, jnp.where(lane == 66, lowest, 0.0)))).astype(BF16))

    by_pairs(g4, context, early_products)
    keep(1, xbuf).start()

    s3 = GroupSum(mlp, *[v[n] for n in ("near2", "sent2", "half2", "full2")], *sems(2))
    for i in range(4):
        s3.give(i)
    def dense_products():
        product(0, 2, v["low_d"], ctx)
        all_d.wait()
        keep(1, xbuf).wait()
        product(26, 2, v["sum_d"], v["cols"].at[1])
        all_n.wait()
        product(30, 2, v["sum_n"], v["cols"].at[3])
        spread.start()

    dense_products()
    hooks_back = {0: s3.far, 1: s3.near_up, 2: s3.near_down, 6: spread.add, 7: spread.deal, 8: s3.pass_on,
                  15: spread.deal_plane}
    dk, dv = v["dact"].at[:, 0:128], v["dact"].at[:, 128:256]

    def head_back(h, carry):
        dk[...] = jnp.zeros_like(dk)
        dv[...] = jnp.zeros_like(dv)
        for i in range(4):
            rows = pl.ds(i * 256, 256)
            q, g = qa[h, rows], grads[h, rows]

            def span(keys, masked):
                k = ka[h, keys]
                score = dot_t(k, q)
                if masked:
                    score = jnp.where(mask, score, MASKED)
                p = jnp.exp(score)
                ds = (p * dot_t(va[h, keys], g)).astype(BF16)
                dk[keys] += dot(ds, q)
                dv[keys] += dot(p.astype(BF16), g)
                return dot_o(k, ds)

            dq = span(rows, True)
            if i:
                dq = dq + span(pl.ds(0, i * 256), False)
            grads[h, rows] = (dq * 0.125).T.astype(BF16)
            for n, hook in hooks_back.items():
                if n % 4 == i:
                    @pl.when(h == n // 4)
                    def _(hook=hook):
                        hook()
        ka[h] = dk[...].astype(BF16)
        va[h] = dv[...].astype(BF16)
        return carry

    lax.fori_loop(0, 4, head_back, 0)
    dfused = v["dfused"]
    for h in (0, 2):
        dfused[:, h * 192:h * 192 + 384] = jnp.concatenate(
            [ref[k, :, :64] for k in (h, h + 1) for ref in (grads, ka, va)], axis=1)

    src[3] = dot_t(pick(pk, "joined_out"), dfused[...]).astype(BF16)
    sum_q = LowSum(src.at[3], got.at[3], *sems(2))
    sum_q.start()
    s4 = GroupSum(*[v[n] for n in ("parts", "near", "sent", "half", "full")], *sems(2))
    s2.finish()
    all_q = LowGather(v["sum_q"], *sems(2))

    def early_low():
        value = sum_q.total()
        all_q.start(value)

    spread2 = LastSpread(split2, whole2, *sems(10))

    def late_products():
        spread2.mark(pk[:8, PICKS["hot"][0]:PICKS["hot"][0] + 128])
        for n in range(0, 6, 2):
            spread2.put(n, dot(v["low_q"][...], dfused[:, n * 128:n * 128 + 256]))

    summed(s4, wide(dfused, v["wj"]), early_low, late_products)
    all_q.wait()
    spread2.put(6, dot(v["sum_q"][...], v["cols"][0]))
    spread2.start()
    layer, mine_grad = v["layer"], v["gos"]
    pairs = [(sub(mine_grad, j), sub(back, j), sub(back, j)) for j in range(4)] + [(layer, out, out)]
    sw2 = Swap(pairs, *sems(3))
    s3.arrive()
    for thing in (g4, s3):
        thing.finish()
    layer[...] = (mid[...] + bias_n[...] + dot_o(v["sum_n"][:, mine_rows], pick(pk, "down_out")) + s3.total()).astype(BF16)
    sw2.start(4)
    spread.share()
    correction = dot_o(v["sum_q"][:, mine_rows], pick(pk, "joined_in"))
    spread2.add()
    spread2.deal()
    s4.arrive()
    for j in ORDER:
        rows = slice(j * 32, (j + 1) * 32)
        value = dmid[rows] + norm_back(xs[rows].astype(F32), gain1[...], correction[rows] + s4.total(rows))
        mine_grad[rows] = value.astype(BF16)
        sw2.start(j)
    spread2.share_groups()
    spread2.line()
    spread.finish()
    spread2.share_line()
    for n in range(5):
        sw2.wait(n)
    spread2.finish()
    for thing in (s4, sw2):
        thing.finish()


SCRATCH = dict(
    lines=((8, 2048), F32), bias=((1, 1024), F32), bias_one=((768,), F32), mine=((16, TRADED), BF16), pk=((16, PICKED), BF16),
    xs=((128, 2048), BF16), xbuf=((1024, 2048), BF16), gbuf=((1024, 2048), BF16), gos=((128, 2048), BF16),
    wj=((2048, 768), BF16), wd=((256, 2048), BF16), wn=((1024, 2048), BF16), wu=((2048, 1024), BF16),
    qa=((4, 1024, 128), BF16), ka=((4, 1024, 128), BF16), va=((4, 1024, 128), BF16), c4=((4, 1024, 128), BF16),
    ctx=((1024, 256), BF16), dfused=((1024, 768), BF16), act=((1024, 1024), BF16),
    dpre=((1024, 1024), BF16), dact=((1024, 1024), F32), mid=((128, 2048), F32), dmid=((128, 2048), F32),
    layer=((128, 2048), BF16), cols=((4, 1024, 256), BF16),
    low_src=((4, 16, 1024), BF16), low_got=((4, 8, 16, 128), BF16),
    low_q=((16, 1024), BF16), low_g=((16, 1024), BF16), low_u=((16, 1024), BF16), low_d=((16, 1024), BF16),
    sum_d=((16, 1024), BF16), sum_u=((16, 1024), BF16), sum_n=((16, 1024), BF16), sum_q=((16, 1024), BF16),
    parts=((1024, 2048), BF16), near=((4, 128, 2048), BF16), sent=((3, 128, 2048), BF16), half=((2, 64, 2048), BF16),
    full=((2, 128, 2048), BF16), near2=((4, 128, 2048), BF16), sent2=((3, 128, 2048), BF16),
    half2=((2, 64, 2048), BF16), full2=((2, 128, 2048), BF16))


def block_call(*args):
    outs = [shape(128, 2048), shape(128, 2048), shape(8, 16, 3, 8, 128), shape(8, 8, 16, 8, 128),
            shape(8, 12, 8, 128), shape(8, 8, 4, 8, 128)]
    low = [DMA((8,)), DMA((8,))]
    sums = [DMA((10,)), DMA((10,))]
    gather = GroupGather.SEMS
    kinds = [DMA((8,)), DMA((8,)), DMA((4,)), *Swap.sems(11), *PlaneGather.SEMS * 4, *gather, *gather, *low, *sums,
             *gather, *low, *low, *sums, *low, *low, *low, *gather, *Spread.SCRATCH, *sums, *low, *sums, *low,
             *LastSpread.SCRATCH, *Swap.sems(5)]
    return pl.pallas_call(
        block_kernel, out_shape=outs, in_specs=specs(pltpu.SMEM, *[ANY] * 22), out_specs=specs(*[ANY] * 6),
        scratch_shapes=[VMEM(*s) for s in SCRATCH.values()] + kinds,
        compiler_params=params(1, 60), name="block")(*args)


def write_kernel(split, whole, split2, whole2, back, layer, *outs):
    joined_out, dense_in, up_out, down_in, *wholes, grad, out = outs
    for ref, count, first in ((dense_in, 2, 0), (up_out, 8, 2), (down_in, 8, 10)):
        for n in range(count):
            for half in (0, 1):
                k = 2 * (first + n) + half
                ref[:, half * 8:half * 8 + 8, n * 128:n * 128 + 128] = split[:, k // 3, k % 3].astype(F32)
    for n in range(6):
        for half in (0, 1):
            joined_out[:, half * 8:half * 8 + 8, n * 128:n * 128 + 128] = split2[:, 2 * n + half].astype(F32)
    for i, ref in enumerate(wholes):
        for t in range(8):
            for n in range(2):
                for half in (0, 1):
                    at = t * 256 + n * 128
                    k = n * 2 + half
                    block_in = whole2[:, t, k] if i == 0 else whole[:, t, i * 4 + k]
                    ref[:, half * 8:half * 8 + 8, at:at + 128] = block_in.astype(F32)
    grad[...] = back[...].astype(F32)
    out[...] = layer[...]


def write_call(split, whole, split2, whole2, back, layer):
    widths = [768, 256, 1024, 1024] + [2048] * 4
    rows = pl.BlockSpec((32, 2048), lambda b: (b, 0))
    return pl.pallas_call(
        write_kernel, grid=(4,),
        out_shape=[shape(8, 16, n, dtype=F32) for n in widths] + [shape(128, 2048, dtype=F32), shape(128, 2048)],
        in_specs=[pl.BlockSpec((2, *n, 8, 128), lambda b, n=n: (b, *[0] * len(n), 0, 0)) for n in ((16, 3), (8, 16), (12,), (8, 4))
                  ] + [rows, rows],
        out_specs=[pl.BlockSpec((2, 16, n), lambda b: (b, 0, 0)) for n in widths] + [rows, rows],
        compiler_params=plain(58), name="write")(split, whole, split2, whole2, back, layer)


def local(tokens, grad_out, adapter_ids, first_gain, first_shift, joined_weight, joined_bias, dense_weight,
          dense_bias, second_gain, second_shift, up_weight, up_bias, down_weight, down_bias, joined_adapt_in,
          joined_adapt_out, dense_adapt_in, dense_adapt_out, up_adapt_in, up_adapt_out, down_adapt_in,
          down_adapt_out):
    turn = lambda a: jnp.swapaxes(a, 1, 2)
    flat = lambda a: a.reshape(128, a.shape[2])
    vectors = [a.reshape(1, -1) for a in (first_gain, first_shift, second_gain, second_shift, dense_bias, down_bias,
                                          up_bias)] + [joined_bias]
    adapters = dict(joined_in=turn(joined_adapt_in), joined_out=joined_adapt_out, dense_in=turn(dense_adapt_in),
                    dense_out=dense_adapt_out, up_in=turn(up_adapt_in), up_out=up_adapt_out,
                    down_in=turn(down_adapt_in), down_out=down_adapt_out)
    back, layer, split, whole, split2, whole2 = block_call(
        adapter_ids, tokens, grad_out, *vectors, *[flat(adapters[n]) for n in SETS], joined_weight, dense_weight,
        down_weight, up_weight)
    joined_out, dense_in, up_out, down_in, joined_in, dense_out, up_in, down_out, grad_tokens, layer_out = write_call(
        split, whole, split2, whole2, back, layer)
    return (layer_out, grad_tokens, turn(joined_in), joined_out, turn(dense_in), dense_out, turn(up_in), up_out,
            turn(down_in), down_out)


def solution(mesh):
    fine = Mesh(mesh.devices.reshape(2, 4, 2, 2, 4), AXES)
    rows, cols = P(FSDP, TP), P(TP, FSDP)
    tok = P((*FSDP, *TP), None)
    last, middle, one = P(None, None, TP), P(None, TP, None), P(TP)
    return jax.shard_map(
        local, mesh=fine,
        in_specs=(tok, tok, P(FSDP), P(), P(), rows, one, cols, P(), P(), P(), rows, one, cols, P(), P(), last,
                  middle, P(), P(), last, middle, P()),
        out_specs=(tok, tok, P(), last, middle, P(), P(), last, middle, P()), check_vma=False)
```

profile of v0, /device:TPU:1, one launch (start us, length us, event | category | flops | bytes accessed | tf_op | source)
XLA Modules:
  0.0 235.9 jit_solution(17893151445341462653)
XLA Ops:
  1.3 228.8 %block.1 = (bf16[128,2048]{1,0:T(8,128)(2,1)}, bf16[128,2048]{1,0:T(8,128)(2,1)}, bf16[8,16,3,8,128]{4,3,2,1,0:T(8,128)(2,1)}, bf16[8,8,16,8,128]{4,3,2,1,0:T(8,...) custom-call(s32[1]{0:T(128)S(6)} %copy.33.refs_0_, bf16[128,2048]{1,0:T(8,128)(2,1)} %refs_1_.1, ...), custom_call_target="tpu_custom_call" | custom-call | tf_op jit(solution)/shard_map/block/pallas_call | solution.py:1343
  230.1 5.6 %write.1 = (f32[8,16,768]{2,1,0:T(8,128)}, f32[8,16,256]{2,1,0:T(8,128)}, f32[8,16,1024]{2,1,0:T(8,128)}, f32[8,16,1024]{2,1,0:T(8,128)}, f32[8,16,2048]{2,1,0:T...) custom-call(bf16[8,16,3,8,128]{4,3,2,1,0:T(8,128)(2,1)} %get-tuple-e, ...), custom_call_target="tpu_custom_call" | custom-call | tf_op jit(solution)/shard_map/write/pallas_call | solution.py:1374
where the time goes:
time: 236 us
  Pallas kernels  234 us (99%)
    pallas_call x1, Pallas kernels, block_call(): pl.pallas_call(block_kernel, out_shape=outs, in_specs=specs(pltpu.SMEM, *...  229 us
    pallas_call x1, Pallas kernels, write_call(): pl.pallas_call(write_kernel, grid=(4,), out_shape=[shape(8, 16, n, dtype=...  5.63 us

commit v1 on v0

--- a/solution.py
+++ b/solution.py
@@ -1096,13 +1096,18 @@
             @pl.when(p == 0)
             def _():
                 g.shared(2)
+                if not beside:
+                    g.near(0)
+                    g.near(3)
 
             @pl.when(p == 1)
             def _():
                 if beside:
                     beside()
-                for j in ORDER:
-                    g.near(j)
+                    g.near(0)
+                    g.near(3)
+                g.near(1)
+                g.near(2)
                 g.shared(6)
 
             @pl.when(p == 2)
@@ -1156,17 +1161,16 @@
     def forward_down(rows):
         mlp[rows] = dot(act[rows], v["wn"][...]).astype(BF16)
 
+    src[2] = dot_t(pick(pk, "down_in"), act[...]).astype(BF16)
+    sum_n = LowSum(src.at[2], got.at[2], *sems(2))
+    sum_n.start()
     tiles(4, 256, forward_down)
-    src[2] = dot_t(pick(pk, "down_in"), act[...]).astype(BF16)
     total_u = sum_u.total()
     dmid[...] = dot_o(total_u, pick(pk, "up_in"))
-    sum_n = LowSum(src.at[2], got.at[2], *sems(2))
-    sum_n.start()
     all_u = LowGather(v["sum_u"], *sems(2))
     all_u.start(total_u)
     s2.arrive()
     all_n = LowGather(v["sum_n"], *sems(2))
-    all_n.start(sum_n.total())
     g4 = GroupGather(xbuf, *sems(2))
     for j in ORDER:
         rows = slice(j * 32, (j + 1) * 32)
@@ -1180,6 +1184,7 @@
             spread.put(first + n, dot(low[...], ref[:, n * 128:n * 128 + 256]))
 
     def early_products():
+        all_n.start(sum_n.total())
         spread.mark(pk[:8, PICKS["hot"][0]:PICKS["hot"][0] + 128])
         product(2, 8, v["low_u"], dpre)
         product(10, 8, v["low_g"], act)
@@ -1304,8 +1309,9 @@
         value = dmid[rows] + norm_back(xs[rows].astype(F32), gain1[...], correction[rows] + s4.total(rows))
         mine_grad[rows] = value.astype(BF16)
         sw2.start(j)
+        if j == 3:
+            spread2.line()
     spread2.share_groups()
-    spread2.line()
     spread.finish()
     spread2.share_line()
     for n in range(5):
@@ -1370,13 +1376,13 @@
 
 def write_call(split, whole, split2, whole2, back, layer):
     widths = [768, 256, 1024, 1024] + [2048] * 4
-    rows = pl.BlockSpec((32, 2048), lambda b: (b, 0))
+    rows = pl.BlockSpec((64, 2048), lambda b: (b, 0))
     return pl.pallas_call(
-        write_kernel, grid=(4,),
+        write_kernel, grid=(2,),
         out_shape=[shape(8, 16, n, dtype=F32) for n in widths] + [shape(128, 2048, dtype=F32), shape(128, 2048)],
-        in_specs=[pl.BlockSpec((2, *n, 8, 128), lambda b, n=n: (b, *[0] * len(n), 0, 0)) for n in ((16, 3), (8, 16), (12,), (8, 4))
+        in_specs=[pl.BlockSpec((4, *n, 8, 128), lambda b, n=n: (b, *[0] * len(n), 0, 0)) for n in ((16, 3), (8, 16), (12,), (8, 4))
                   ] + [rows, rows],
-        out_specs=[pl.BlockSpec((2, 16, n), lambda b: (b, 0, 0)) for n in widths] + [rows, rows],
+        out_specs=[pl.BlockSpec((4, 16, n), lambda b: (b, 0, 0)) for n in widths] + [rows, rows],
         compiler_params=plain(58), name="write")(split, whole, split2, whole2, back, layer)
 
 

time: 236 us -> 233 us (0.987)
  no operation moved by 1% of the time
where the time goes in v1:
time: 233 us
  Pallas kernels  232 us (100%)
    pallas_call x1, Pallas kernels, block_call(): pl.pallas_call(block_kernel, out_shape=outs, in_specs=specs(pltpu.SMEM, *...  227 us
    pallas_call x1, Pallas kernels, write_call(): pl.pallas_call(write_kernel, grid=(2,), out_shape=[shape(8, 16, n, dtype=...  4.77 us

profile of v1, /device:TPU:1, one launch (start us, length us, event | category | flops | bytes accessed | tf_op | source)
XLA Modules:
  0.0 233.3 jit_solution(7049458717925151480)
XLA Ops:
  1.3 227.0 %block.1 = (bf16[128,2048]{1,0:T(8,128)(2,1)}, bf16[128,2048]{1,0:T(8,128)(2,1)}, bf16[8,16,3,8,128]{4,3,2,1,0:T(8,128)(2,1)}, bf16[8,8,16,8,128]{4,3,2,1,0:T(8,...) custom-call(s32[1]{0:T(128)S(6)} %copy.33.refs_0_, bf16[128,2048]{1,0:T(8,128)(2,1)} %refs_1_.1, ...), custom_call_target="tpu_custom_call" | custom-call | tf_op jit(solution)/shard_map/block/pallas_call | solution.py:1349
  228.3 4.8 %write.1 = (f32[8,16,768]{2,1,0:T(8,128)}, f32[8,16,256]{2,1,0:T(8,128)}, f32[8,16,1024]{2,1,0:T(8,128)}, f32[8,16,1024]{2,1,0:T(8,128)}, f32[8,16,2048]{2,1,0:T...) custom-call(bf16[8,16,3,8,128]{4,3,2,1,0:T(8,128)(2,1)} %get-tuple-e, ...), custom_call_target="tpu_custom_call" | custom-call | tf_op jit(solution)/shard_map/write/pallas_call | solution.py:1380

commit v2 on v1

--- a/solution.py
+++ b/solution.py
@@ -914,12 +914,12 @@
     low_pair(lax.rem(z + 3, 4))
     g1.shared(6)
     low_pair(lax.rem(z + 1, 4))
+    for n in (5, 6):
+        sw.wait(n)
+    joined.wait()
     g1.shared(7)
     low_pair(lax.rem(z + 2, 4))
     g2 = GroupGather(gbuf, *sems(2))
-    for n in (5, 6):
-        sw.wait(n)
-    joined.wait()
 
     lane = lax.broadcasted_iota(jnp.int32, (256, 128), 1)
     row = lax.broadcasted_iota(jnp.int32, (256, 128), 0)

time: 233 us -> 233 us (level)
  no operation moved by 1% of the time
where the time goes in v2:
time: 233 us
  Pallas kernels  232 us (100%)
    pallas_call x1, Pallas kernels, block_call(): pl.pallas_call(block_kernel, out_shape=outs, in_specs=specs(pltpu.SMEM, *...  227 us
    pallas_call x1, Pallas kernels, write_call(): pl.pallas_call(write_kernel, grid=(2,), out_shape=[shape(8, 16, n, dtype=...  4.77 us

profile of v2, /device:TPU:1, one launch (start us, length us, event | category | flops | bytes accessed | tf_op | source)
XLA Modules:
  0.0 233.3 jit_solution(4865564844294642551)
XLA Ops:
  1.3 227.0 %block.1 = (bf16[128,2048]{1,0:T(8,128)(2,1)}, bf16[128,2048]{1,0:T(8,128)(2,1)}, bf16[8,16,3,8,128]{4,3,2,1,0:T(8,128)(2,1)}, bf16[8,8,16,8,128]{4,3,2,1,0:T(8,...) custom-call(s32[1]{0:T(128)S(6)} %copy.33.refs_0_, bf16[128,2048]{1,0:T(8,128)(2,1)} %refs_1_.1, ...), custom_call_target="tpu_custom_call" | custom-call | tf_op jit(solution)/shard_map/block/pallas_call | solution.py:1349
  228.3 4.8 %write.1 = (f32[8,16,768]{2,1,0:T(8,128)}, f32[8,16,256]{2,1,0:T(8,128)}, f32[8,16,1024]{2,1,0:T(8,128)}, f32[8,16,1024]{2,1,0:T(8,128)}, f32[8,16,2048]{2,1,0:T...) custom-call(bf16[8,16,3,8,128]{4,3,2,1,0:T(8,128)(2,1)} %get-tuple-e, ...), custom_call_target="tpu_custom_call" | custom-call | tf_op jit(solution)/shard_map/write/pallas_call | solution.py:1380
